TPU v7x, 32 devices: a whole 2x2x4 slice. The times are simulated.
32 devices in a mesh: replica: 8 (over z, core), tensor: 4 (over y, x).
Axes of the slice: x: 2, y: 2, z: 4, core: 2. Of those that a mesh axis runs over, the one named last changes fastest.
Arguments:
- hidden: bfloat16 [3, 64, 8192], P(None, None, 'replica'), may hold values from -6 to 6
- parents: int32 [3, 64], replicated, may hold values from 0 to 63, as said below
- input_weight: bfloat16 [8192, 2, 8192], P('replica', None, 'tensor'), may hold values from -0.0625 to 0.0625
- coeff_weight: bfloat16 [8192, 2, 512], P('replica'), may hold values from -0.0625 to 0.0625
- step_weight: bfloat16 [8192, 128], P('replica', 'tensor'), may hold values from -0.0625 to 0.0625
- kernel_x: float32 [4, 8192], P(None, 'tensor'), may hold values from -0.5 to 0.5
- kernel_bias_x: float32 [8192], P('tensor'), may hold values from -0.5 to 0.5
- kernel_coeff: float32 [4, 2, 512], replicated, may hold values from -0.5 to 0.5
- kernel_bias_coeff: float32 [2, 512], replicated, may hold values from -0.5 to 0.5
- step_bias: float32 [128], P('tensor'), may hold values from -3 to 0
- log_rate: float32 [128], P('tensor'), may hold values from -4 to 0.7
- skip_gain: float32 [128], P('tensor'), may hold values from 0.5 to 2
- norm_gain: float32 [8192], P('tensor'), may hold values from 0.1 to 1.9
- output_weight: bfloat16 [8192, 8192], P('tensor', 'replica'), may hold values from -0.0625 to 0.0625
- scan_state: float32 [64, 128, 64, 128], P('replica', 'tensor'), may hold values from -6 to 6
- window_x: float32 [64, 3, 8192], P('replica', None, 'tensor'), may hold values from -6 to 6
- window_coeff: float32 [64, 3, 2, 512], P('replica'), may hold values from -6 to 6
Outputs:
- mixed_out: bfloat16 [3, 64, 8192], P(None, 'tensor', 'replica')
- final_state: float32 [64, 128, 64, 128], P('replica', 'tensor')
- final_window_x: float32 [64, 3, 8192], P('replica', None, 'tensor')
- final_window_coeff: float32 [64, 3, 2, 512], P('replica')
Inputs may be any that keep to these rules, and one draw needn't show every extreme that they name: On each step, of the 8 rows of one replica (rows of one aligned block of 8), exactly one has its parent on that same replica; two share one parent on another replica; each of the other 5 has its parent on yet another replica, all these replicas distinct. So no other replica holds the parents of more than 2 rows of one replica, nor more than one distinct parent of them. Rows within a block come in any order.
All inputs are finite; a program needn't handle non-finite values.
Results may differ from a plain program's by a relative error of at most 0.005.
Values may be sent and summed in bfloat16 or wider, within the bound.
A program may use at most 192 MiB of HBM per device.

v0:
```python
import jax
import jax.numpy as jnp
from jax import lax
from jax.sharding import PartitionSpec as P


def route(parent_row, rows_dev, replicas, my_replica, slots):
    grid = parent_row.reshape(replicas, rows_dev)
    source = grid // rows_dev
    local_row = grid % rows_dev
    dest_replica = jnp.arange(replicas, dtype=jnp.int32)[:, None]
    remote = source != dest_replica
    matched = remote & (source == my_replica)
    own_source = lax.dynamic_index_in_dim(source, my_replica, 0, keepdims=False)
    own_local = lax.dynamic_index_in_dim(local_row, my_replica, 0, keepdims=False)
    own_remote = lax.dynamic_index_in_dim(remote, my_replica, 0, keepdims=False)
    sending = jnp.max(jnp.where(matched, local_row, 0), axis=1)[:, None]
    fetch_rows = jnp.where(own_remote, rows_dev + own_source * slots, own_local)
    return (sending, fetch_rows)


def local(
    hidden,
    parents,
    input_weight,
    coeff_weight,
    step_weight,
    kernel_x,
    kernel_bias_x,
    kernel_coeff,
    kernel_bias_coeff,
    step_bias,
    log_rate,
    skip_gain,
    norm_gain,
    output_weight,
    scan_state,
    window_x,
    window_coeff,
):
    rows_dev, heads_dev, head_dim, state_dim = scan_state.shape
    replicas = lax.axis_size("replica")
    my_replica = lax.axis_index("replica")
    my_tensor = lax.axis_index("tensor")
    heads_all = heads_dev * lax.axis_size("tensor")
    groups = kernel_bias_coeff.shape[1] // state_dim
    group_size = heads_all * head_dim // groups
    head_ids = my_tensor * heads_dev + jnp.arange(heads_dev, dtype=jnp.int32)
    coeff_group = head_ids * groups // heads_all
    member = (coeff_group[:, None] == jnp.arange(groups, dtype=jnp.int32)[None, :]).astype(
        jnp.float32
    )
    norm_group = head_ids % groups
    norm_member = (norm_group[:, None] == jnp.arange(groups, dtype=jnp.int32)[None, :]).astype(
        jnp.float32
    )
    rate = jnp.exp(log_rate)
    gains = norm_gain.reshape(heads_dev, head_dim)
    slots = 1
    results = []
    for step_index in range(hidden.shape[0]):
        sending, fetch_rows = route(parents[step_index], rows_dev, replicas, my_replica, slots)
        flat_rows = sending.reshape(-1)
        sent_state = jnp.take(scan_state, flat_rows, axis=0).reshape(
            (replicas, slots) + scan_state.shape[1:]
        )
        sent_x = jnp.take(window_x, flat_rows, axis=0).reshape(
            (replicas, slots) + window_x.shape[1:]
        )
        sent_coeff = jnp.take(window_coeff, flat_rows, axis=0).reshape(
            (replicas, slots) + window_coeff.shape[1:]
        )
        arrived = (
            lax.all_to_all(sent_state, "replica", split_axis=0, concat_axis=0, tiled=True),
            lax.all_to_all(sent_x, "replica", split_axis=0, concat_axis=0, tiled=True),
            lax.all_to_all(sent_coeff, "replica", split_axis=0, concat_axis=0, tiled=True),
        )
        held_states = (scan_state, window_x, window_coeff)
        moved = []
        for held, came in zip(held_states, arrived):
            joined = jnp.concatenate(
                [held, came.reshape((replicas * slots,) + held.shape[1:])], axis=0
            )
            moved.append(jnp.take(joined, fetch_rows, axis=0))
        scan_state, window_x, window_coeff = (moved[0], moved[1], moved[2])
        step_input = hidden[step_index]
        gate_x = jnp.einsum(
            "rd,dkc->rkc", step_input, input_weight, preferred_element_type=jnp.float32
        )
        coeffs = jnp.einsum(
            "rd,dkc->rkc", step_input, coeff_weight, preferred_element_type=jnp.float32
        )
        step_raw = jnp.dot(step_input, step_weight, preferred_element_type=jnp.float32)
        gate_x, coeffs, step_raw = (
            lax.psum_scatter(gate_x, "replica", scatter_dimension=0, tiled=True),
            lax.psum_scatter(coeffs, "replica", scatter_dimension=0, tiled=True),
            lax.psum_scatter(step_raw, "replica", scatter_dimension=0, tiled=True),
        )
        full_x = jnp.concatenate([window_x, gate_x[:, 1][:, None]], axis=1)
        mixed_x = jax.nn.silu(jnp.sum(full_x * kernel_x[None], axis=1) + kernel_bias_x)
        window_x = full_x[:, 1:]
        full_coeff = jnp.concatenate([window_coeff, coeffs[:, None]], axis=1)
        mixed_coeff = jax.nn.silu(
            jnp.sum(full_coeff * kernel_coeff[None], axis=1) + kernel_bias_coeff
        )
        window_coeff = full_coeff[:, 1:]
        step_size = jax.nn.softplus(step_raw + step_bias)
        decay = jnp.exp(-rate * step_size)
        heads_x = mixed_x.reshape(rows_dev, heads_dev, head_dim)
        input_b = jnp.einsum(
            "rgn,hg->rhn",
            mixed_coeff[:, 0].reshape(rows_dev, groups, state_dim),
            member,
            precision=lax.Precision.HIGHEST,
        )
        output_c = jnp.einsum(
            "rgn,hg->rhn",
            mixed_coeff[:, 1].reshape(rows_dev, groups, state_dim),
            member,
            precision=lax.Precision.HIGHEST,
        )
        scan_state = (
            decay[:, :, None, None] * scan_state
            + (step_size[:, :, None] * heads_x)[..., None] * input_b[:, :, None, :]
        )
        heads_y = (
            jnp.sum(scan_state * output_c[:, :, None, :], axis=-1)
            + skip_gain[None, :, None] * heads_x
        )
        heads_y = heads_y * jax.nn.silu(gate_x[:, 0].reshape(rows_dev, heads_dev, head_dim))
        squares = jnp.dot(
            jnp.sum(heads_y * heads_y, axis=-1), norm_member, precision=lax.Precision.HIGHEST
        )
        squares = lax.psum(squares, "tensor")
        inverse = lax.rsqrt(squares / group_size + 1e-05)
        head_scale = jnp.dot(inverse, norm_member.T, precision=lax.Precision.HIGHEST)
        normed = (
            (heads_y * head_scale[:, :, None] * gains[None])
            .reshape(rows_dev, heads_dev * head_dim)
            .astype(jnp.bfloat16)
        )
        mixed_all = jnp.dot(
            lax.all_gather(normed, "replica", axis=0, tiled=True),
            output_weight,
            preferred_element_type=jnp.float32,
        )
        results.append(
            lax.psum_scatter(mixed_all, "tensor", scatter_dimension=0, tiled=True).astype(
                jnp.bfloat16
            )
        )
    return (jnp.stack(results), scan_state, window_x, window_coeff)


def solution(mesh):
    placed = (
        P(None, None, "replica"),
        P(),
        P("replica", None, "tensor"),
        P("replica", None, None),
        P("replica", "tensor"),
        P(None, "tensor"),
        P("tensor"),
        P(),
        P(),
        P("tensor"),
        P("tensor"),
        P("tensor"),
        P("tensor"),
        P("tensor", "replica"),
        P("replica", "tensor", None, None),
        P("replica", None, "tensor"),
        P("replica", None, None, None),
    )
    return jax.shard_map(
        local,
        mesh=mesh,
        in_specs=placed,
        out_specs=(
            P(None, "tensor", "replica"),
            P("replica", "tensor", None, None),
            P("replica", None, "tensor"),
            P("replica", None, None, None),
        ),
        check_vma=False,
    )
```

profile of v0, /device:TPU:0, one launch (start us, length us, event | category | flops | bytes accessed | tf_op | source)
XLA Modules:
  0.0 1014.4 jit_solution(7893398277149278962)
XLA Ops:
  13.1 9.3 fusion.7
  24.1 6.4 all-to-all-start.2
  30.7 9.3 fusion.5
  43.1 7.9 gather_fusion
  56.9 8.1 all-to-all-done.1
  80.8 28.9 %reduce-scatter.10.cloned.1.call-done = f32[8,2,2048]{2,0,1:T(8,128)} async-done(((f32[64,2,2048]{2,0,1:T(8,128)}), f32[8,2,2048]{2,0,1:T(8,128)}) %reduce-scatter.10.cloned.1.call-update) | async-done | bytes 131088 | tf_op jit(solution)/shard_map/reduce_scatter | solution.py:95
  116.6 26.1 %reduce-scatter.16.cloned.1.call-done = f32[8,2,2048]{2,0,1:T(8,128)} async-done(((f32[64,2,2048]{2,0,1:T(8,128)}), f32[8,2,2048]{2,0,1:T(8,128)}) %reduce-scatter.16.cloned.1.call-update) | async-done | bytes 131088 | tf_op jit(solution)/shard_map/reduce_scatter | solution.py:95
  158.7 8.8 select_bitcast_fusion.2
  167.4 5.4 all-to-all-start
  175.1 9.3 fusion.3
  188.9 195.6 %all-reduce.3 = (f32[64,32]{1,0:T(8,128)S(1)}, f32[64,32]{1,0:T(8,128)S(1)}, f32[64,32]{1,0:T(8,128)S(1)}) all-reduce(f32[64,32]{1,0:T(8,128)S(1)} %fusion.37, f32[64,32]{1,0:T(8,128)S(1)} %fusion.33, f32[64,32]{1,0:T(8,128)S(1)} %fusion.29), channel_id=2, replica_groups=mesh['replica'=8,'tensor'=4] {'replica'}, use_global_device_ids=true, to_apply=%region_0.1.clone | all-reduce | flops 6144 | bytes 49152
  395.0 11.9 %pad_maximum_fusion = f32[16,32,64,128]{3,2,1,0:T(8,128)} fusion(f32[8,32,64,128]{3,2,1,0:T(8,128)} %bitcast.3, f32[8,32,64,128]{3,2,1,0:T(8,128)} %param.43), kind=kLoop, calls=%fused_computation.18 | loop fusion | flops 4194304 | bytes 33554432 | tf_op jit(solution)/shard_map/concatenate | solution.py:81
  406.9 10.4 %gather_fusion.1 = f32[8,32,64,128]{3,2,1,0:T(8,128)} fusion(f32[16,32,64,128]{3,2,1,0:T(8,128)} %pad_maximum_fusion, s32[1024]{0:T(1024)} %copy-done.21), kind=kCustom, calls=%fused_computation.1.clone | custom fusion | bytes 16777248 | tf_op jit(solution)/shard_map/jit(_take)/gather | solution.py:84
  417.3 9.2 multiply_reduce_fusion.2
  426.5 7.8 gather_fusion.6
  434.3 8.6 select_bitcast_fusion.1
  448.4 183.3 %all-to-all-done.3 = f32[8,1,32,64,128]{4,3,2,1,0:T(8,128)} async-done(((f32[8,1,32,64,128]{4,3,2,1,0:T(8,128)}), f32[8,1,32,64,128]{4,3,2,1,0:T(8,128)}, u32[]{:S(2)}, u32[]{:S(2)}) %all-to-all-start.3) | async-done | bytes 8388640 | tf_op jit(solution)/shard_map/all_to_all | solution.py:74
  631.7 11.9 %pad_maximum_fusion.1 = f32[16,32,64,128]{3,2,1,0:T(8,128)} fusion(f32[8,32,64,128]{3,2,1,0:T(8,128)} %bitcast.21, f32[8,32,64,128]{3,2,1,0:T(8,128)} %get-tuple-element.57), kind=kLoop, calls=%fused_computation.19 | loop fusion | flops 4194304 | bytes 33554432 | tf_op jit(solution)/shard_map/concatenate | solution.py:81
  643.5 10.4 %gather_fusion.7 = f32[8,32,64,128]{3,2,1,0:T(8,128)} fusion(f32[16,32,64,128]{3,2,1,0:T(8,128)} %pad_maximum_fusion.1, s32[1024]{0:T(1024)} %copy-done.19), kind=kCustom, calls=%fused_computation.8.clone | custom fusion | bytes 16777248 | tf_op jit(solution)/shard_map/jit(_take)/gather | solution.py:84
  653.9 9.2 multiply_reduce_fusion.1
  663.1 7.8 gather_fusion.12
  670.9 8.6 select_bitcast_fusion
  686.0 182.6 %all-to-all-done.6 = f32[8,1,32,64,128]{4,3,2,1,0:T(8,128)} async-done(((f32[8,1,32,64,128]{4,3,2,1,0:T(8,128)}), f32[8,1,32,64,128]{4,3,2,1,0:T(8,128)}, u32[]{:S(2)}, u32[]{:S(2)}) %all-to-all-start.6) | async-done | bytes 8388640 | tf_op jit(solution)/shard_map/all_to_all | solution.py:74
  868.6 11.9 %pad_maximum_fusion.2 = f32[16,32,64,128]{3,2,1,0:T(8,128)} fusion(f32[8,32,64,128]{3,2,1,0:T(8,128)} %bitcast.39, f32[8,32,64,128]{3,2,1,0:T(8,128)} %get-tuple-element.53), kind=kLoop, calls=%fused_computation.20 | loop fusion | flops 4194304 | bytes 33554432 | tf_op jit(solution)/shard_map/concatenate | solution.py:81
  880.5 10.2 %gather_fusion.13 = f32[8,32,64,128]{3,2,1,0:T(8,128)} fusion(f32[16,32,64,128]{3,2,1,0:T(8,128)} %pad_maximum_fusion.2, s32[1024]{0:T(1024)S(1)} %pad_clamp_fusion), kind=kCustom, calls=%fused_computation.9.clone | custom fusion | bytes 16777248 | tf_op jit(solution)/shard_map/jit(_take)/gather | solution.py:84
  890.7 9.2 multiply_reduce_fusion
  901.2 9.7 all-reduce.4
  912.3 14.3 %all_gather.11 = bf16[64,2048]{1,0:T(8,128)(2,1)S(1)} all-gather(bf16[8,2048]{1,0:T(8,128)(2,1)S(1)} %get-tuple-element.89), channel_id=1, replica_groups=mesh['replica'=8,'tensor'=4] {'replica'}, dimensions={0}, use_global_device_ids=true | all-gather | bytes 294912 | tf_op jit(solution)/shard_map/all_gather | solution.py:143
  930.4 14.3 %all_gather.10 = bf16[64,2048]{1,0:T(8,128)(2,1)S(1)} all-gather(bf16[8,2048]{1,0:T(8,128)(2,1)S(1)} %get-tuple-element.88), channel_id=1, replica_groups=mesh['replica'=8,'tensor'=4] {'replica'}, dimensions={0}, use_global_device_ids=true | all-gather | bytes 294912 | tf_op jit(solution)/shard_map/all_gather | solution.py:143
  949.2 14.2 %all_gather.9 = bf16[64,2048]{1,0:T(8,128)(2,1)S(1)} all-gather(bf16[8,2048]{1,0:T(8,128)(2,1)S(1)} %get-tuple-element.87), channel_id=1, replica_groups=mesh['replica'=8,'tensor'=4] {'replica'}, dimensions={0}, use_global_device_ids=true | all-gather | bytes 294912 | tf_op jit(solution)/shard_map/all_gather | solution.py:143
  968.9 10.1 reduce-scatter.20.cloned.1.call-done
  979.9 26.3 %reduce-scatter.14.cloned.1.call-done = f32[16,1024]{1,0:T(8,128)} async-done(((f32[64,1024]{1,0:T(8,128)}), f32[16,1024]{1,0:T(8,128)}) %reduce-scatter.14.cloned.1.call-update) | async-done | bytes 65552 | tf_op jit(solution)/shard_map/reduce_scatter | solution.py:148
  (228 shorter events, 101.9 us)
Async XLA Ops:
  7.2 58.8 %reduce-scatter.12.cloned.1.call-start = ((), (), s32[]{:S(2)}) async-start(), calls=%async_computation.19 | async-start | bytes 294912 | tf_op jit(solution)/shard_map/reduce_scatter | solution.py:96
  10.9 65.3 %reduce-scatter.18.cloned.1.call-start = ((), (), s32[]{:S(2)}) async-start(), calls=%async_computation.22 | async-start | bytes 294912 | tf_op jit(solution)/shard_map/reduce_scatter | solution.py:96
  13.0 96.7 %reduce-scatter.10.cloned.1.call-start = ((), (), s32[]{:S(2)}) async-start(), calls=%async_computation.18 | async-start | bytes 1179648 | tf_op jit(solution)/shard_map/reduce_scatter | solution.py:95
  24.1 26.9 %all-to-all-start.2 = ((f32[8,1,3,2,512]{4,3,2,1,0:T(2,128)}), f32[8,1,3,2,512]{4,3,2,1,0:T(2,128)S(1)}, u32[]{:S(2)}, u32[]{:S(2)}) async-start(f32[8,1,3,2,512]{4,3,2,1,0:T(2,128)} %select_bitcast_fusion.8), calls=%async_computation.3 | async-start | bytes 196608 | tf_op jit(solution)/shard_map/all_to_all | solution.py:76
  30.4 112.3 %reduce-scatter.16.cloned.1.call-start = ((), (), s32[]{:S(2)}) async-start(), calls=%async_computation.21 | async-start | bytes 1179648 | tf_op jit(solution)/shard_map/reduce_scatter | solution.py:95
  42.0 70.2 %copy-start.24 = (pred[8]{0:T(512)(128)(4,1)}, pred[8]{0:T(512)(128)(4,1)S(1)}, u32[]{:S(2)}) copy-start(pred[8]{0:T(512)(128)(4,1)S(1)} %compare_and_fusion.3) | copy-start | bytes 28
  42.0 23.3 %copy-start.21 = (s32[1024]{0:T(1024)}, s32[1024]{0:T(1024)S(1)}, u32[]{:S(2)}) copy-start(s32[1024]{0:T(1024)S(1)} %pad_clamp_fusion.4) | copy-start | bytes 12292
  43.0 68.5 %copy-start.20 = (s32[1024]{0:T(1024)}, s32[1024]{0:T(1024)S(1)}, u32[]{:S(2)}) copy-start(s32[1024]{0:T(1024)S(1)} %pad_clamp_fusion.3) | copy-start | bytes 12292
  43.0 106.3 %copy-start.19 = (s32[1024]{0:T(1024)}, s32[1024]{0:T(1024)S(1)}, u32[]{:S(2)}) copy-start(s32[1024]{0:T(1024)S(1)} %pad_clamp_fusion.2) | copy-start | bytes 12292
  43.1 108.1 %copy-start.18 = (s32[1024]{0:T(1024)}, s32[1024]{0:T(1024)S(1)}, u32[]{:S(2)}) copy-start(s32[1024]{0:T(1024)S(1)} %pad_clamp_fusion.1) | copy-start | bytes 12292
  51.0 116.5 %copy-start.22 = (pred[8]{0:T(512)(128)(4,1)}, pred[8]{0:T(512)(128)(4,1)S(1)}, u32[]{:S(2)}) copy-start(pred[8]{0:T(512)(128)(4,1)S(1)} %compare_and_fusion.1) | copy-start | bytes 28
  51.0 13.9 %all-to-all-start.1 = ((f32[8,1,3,2048]{3,1,2,0:T(1,128)}), f32[8,1,3,2048]{3,1,2,0:T(1,128)S(1)}, u32[]{:S(2)}, u32[]{:S(2)}) async-start(f32[8,1,3,2048]{3,1,2,0:T(1,128)} %copy.115), calls=%async_computation.1 | async-start | bytes 393216 | tf_op jit(solution)/shard_map/all_to_all | solution.py:75
  68.9 9.6 all-to-all-start.5
  76.9 34.3 %copy-start.9 = (f32[8,1,2,512]{3,2,1,0:T(2,128)}, f32[8,1,2,512]{3,2,1,0:T(2,128)S(1)}, u32[]{:S(2)}) copy-start(f32[8,1,2,512]{3,2,1,0:T(2,128)S(1)} %copy.131) | copy-start | bytes 98308
  113.2 31.7 %all-to-all-start.4 = ((f32[8,1,3,2048]{3,1,2,0:T(1,128)}), f32[8,1,3,2048]{3,1,2,0:T(1,128)S(1)}, u32[]{:S(2)}, u32[]{:S(2)}) async-start(f32[8,1,3,2048]{3,1,2,0:T(1,128)} %copy.124), calls=%async_computation.7 | async-start | bytes 393216 | tf_op jit(solution)/shard_map/all_to_all | solution.py:75
  144.9 10.3 %all-to-all-start.8 = ((f32[8,1,3,2,512]{4,3,2,1,0:T(2,128)}), f32[8,1,3,2,512]{4,3,2,1,0:T(2,128)}, u32[]{:S(2)}, u32[]{:S(2)}) async-start(f32[8,1,3,2,512]{4,3,2,1,0:T(2,128)} %select_bitcast_fusion.6), calls=%async_computation.15 | async-start | bytes 196608 | tf_op jit(solution)/shard_map/all_to_all | solution.py:76
  155.3 12.2 %all-to-all-start.7 = ((f32[8,1,3,2048]{3,1,2,0:T(1,128)}), f32[8,1,3,2048]{3,1,2,0:T(1,128)S(1)}, u32[]{:S(2)}, u32[]{:S(2)}) async-start(f32[8,1,3,2048]{3,1,2,0:T(1,128)} %copy.133), calls=%async_computation.13 | async-start | bytes 393216 | tf_op jit(solution)/shard_map/all_to_all | solution.py:75
  167.4 227.6 %all-to-all-start = ((f32[8,1,32,64,128]{4,3,2,1,0:T(8,128)}), f32[8,1,32,64,128]{4,3,2,1,0:T(8,128)}, u32[]{:S(2)}, u32[]{:S(2)}) async-start(f32[8,1,32,64,128]{4,3,2,1,0:T(8,128)} %select_bitcast_fusion.2), calls=%async_computation | async-start | bytes 16777216 | tf_op jit(solution)/shard_map/all_to_all | solution.py:74
  172.8 213.7 %reduce-scatter.24.cloned.1.call-start = ((), (), s32[]{:S(2)}) async-start(), calls=%async_computation.25 | async-start | bytes 294912 | tf_op jit(solution)/shard_map/reduce_scatter | solution.py:96
  175.0 217.6 %copy-start.4 = (f32[8,1,3,2048]{3,1,2,0:T(1,128)S(1)}, f32[8,1,3,2048]{3,1,2,0:T(1,128)}, u32[]{:S(2)}) copy-start(f32[8,1,3,2048]{3,1,2,0:T(1,128)} %copy-done.3) | copy-start | bytes 589828
  175.0 218.8 %copy-start.5 = (f32[8,1,2048]{2,1,0:T(1,128)S(1)}, f32[8,1,2048]{2,1,0:T(1,128)}, u32[]{:S(2)}) copy-start(f32[8,1,2048]{2,1,0:T(1,128)} %copy.128) | copy-start | bytes 196612
  175.0 218.8 %copy-start.16 = (f32[4,2048]{1,0:T(4,128)S(1)}, f32[4,2048]{1,0:T(4,128)}, u32[]{:S(2)}) copy-start(f32[4,2048]{1,0:T(4,128)} %param.34) | copy-start | bytes 98308
  175.0 216.6 %reduce-scatter.22.cloned.1.call-start = ((), (), s32[]{:S(2)}) async-start(), calls=%async_computation.24 | async-start | bytes 1179648 | tf_op jit(solution)/shard_map/reduce_scatter | solution.py:95
  442.9 188.8 %all-to-all-start.3 = ((f32[8,1,32,64,128]{4,3,2,1,0:T(8,128)}), f32[8,1,32,64,128]{4,3,2,1,0:T(8,128)}, u32[]{:S(2)}, u32[]{:S(2)}) async-start(f32[8,1,32,64,128]{4,3,2,1,0:T(8,128)} %select_bitcast_fusion.1), calls=%async_computation.6 | async-start | bytes 16777216 | tf_op jit(solution)/shard_map/all_to_all | solution.py:74
  679.5 189.1 %all-to-all-start.6 = ((f32[8,1,32,64,128]{4,3,2,1,0:T(8,128)}), f32[8,1,32,64,128]{4,3,2,1,0:T(8,128)}, u32[]{:S(2)}, u32[]{:S(2)}) async-start(f32[8,1,32,64,128]{4,3,2,1,0:T(8,128)} %select_bitcast_fusion), calls=%async_computation.12 | async-start | bytes 16777216 | tf_op jit(solution)/shard_map/all_to_all | solution.py:74
  684.8 283.3 %reduce-scatter.26.cloned.1.call-start = ((), (), s32[]{:S(2)}) async-start(), calls=%async_computation.26 | async-start | bytes 327680 | tf_op jit(solution)/shard_map/reduce_scatter | solution.py:148
  890.7 21.4 %copy-start.11 = (f32[8,2,2048]{2,0,1:T(8,128)S(1)}, f32[8,2,2048]{2,0,1:T(8,128)}, u32[]{:S(2)}) copy-start(f32[8,2,2048]{2,0,1:T(8,128)} %reduce-scatter.16.cloned.1.call-done) | copy-start | bytes 393220
  890.7 21.4 %copy-start.12 = (f32[8,2,2048]{2,0,1:T(8,128)S(1)}, f32[8,2,2048]{2,0,1:T(8,128)}, u32[]{:S(2)}) copy-start(f32[8,2,2048]{2,0,1:T(8,128)} %reduce-scatter.22.cloned.1.call-done) | copy-start | bytes 393220
  890.7 21.4 %copy-start.17 = (f32[2048]{0:T(1024)S(1)}, f32[2048]{0:T(1024)}, u32[]{:S(2)}) copy-start(f32[2048]{0:T(1024)} %param.41) | copy-start | bytes 24580
  912.3 95.4 %copy-start.1 = (bf16[1024,2,512]{2,1,0:T(2,128)(2,1)S(1)}, bf16[1024,2,512]{2,1,0:T(2,128)(2,1)}, u32[]{:S(2)}) copy-start(bf16[1024,2,512]{2,1,0:T(2,128)(2,1)} %param.32) | copy-start | bytes 6291460
  930.4 48.7 %reduce-scatter.20.cloned.1.call-start = ((), (), s32[]{:S(2)}) async-start(), calls=%async_computation.23 | async-start | bytes 327680 | tf_op jit(solution)/shard_map/reduce_scatter | solution.py:148
  948.5 57.7 %reduce-scatter.14.cloned.1.call-start = ((), (), s32[]{:S(2)}) async-start(), calls=%async_computation.20 | async-start | bytes 327680 | tf_op jit(solution)/shard_map/reduce_scatter | solution.py:148
  (15 other events, 146.8 us)
Sparse Core Ops, SparseCore 0:
  11.0 33.7 reduce-scatter.11
  47.0 29.1 reduce-scatter.17
  78.4 31.2 reduce-scatter.9
  111.9 30.8 reduce-scatter.15
  175.6 36.6 reduce-scatter.23
  214.4 46.2 reduce-scatter.21
  930.5 21.4 reduce-scatter.25
  954.7 24.3 reduce-scatter.19
  981.8 24.3 reduce-scatter.13
where the time goes:
time: 1030 us; the launch traced here: 1010 us
  waiting for transfers between devices  473 us (46%)
  blocking collectives  248 us (24%)
  other arithmetic  106 us (10%)
  local copies, waits for them, and re-layouts  78.8 us (8%)
  matrix products  51.3 us (5%)
  starting transfers between devices  41.6 us (4%)
  between operations  15.6 us (2%)
    all_to_all x3, waiting for transfers between devices, local(): lax.all_to_all(sent_state, 'replica', split_axis=0, concat_axis=0, tiled=...  366 us
    unnamed x1, blocking collectives  196 us
    reduce_scatter x3, waiting for transfers between devices, local(): lax.psum_scatter(gate_x, 'replica', scatter_dimension=0, tiled=True)  55.1 us
    all_gather x3, blocking collectives, local(): lax.all_gather(normed, 'replica', axis=0, tiled=True)  42.8 us
    concatenate x9, other arithmetic, local(): jnp.concatenate([held, came.reshape((replicas * slots,) + held.shape[1:])...  37.1 us
    reduce_scatter x3, waiting for transfers between devices, local(): lax.psum_scatter(mixed_all, 'tensor', scatter_dimension=0, tiled=True)  36.4 us
    gather x9, local copies, waits for them, and re-layouts, local(): moved.append(jnp.take(joined, fetch_rows, axis=0))  35.1 us
    dot_general x3, matrix products, local(): jnp.einsum('rd,dkc->rkc', step_input, input_weight, preferred_element_typ...  28 us
  transfers between devices with their start and end apart: 18, of which 10 were waited for; matrix products, arithmetic and copies ran while one was open for 10% of the time, Pallas kernels for 0%

commit v1 on v0

v1 whole, which is shorter than its diff:
```python
import jax
import jax.numpy as jnp
from jax import lax
from jax.sharding import PartitionSpec as P

BF = jnp.bfloat16
F32 = jnp.float32


def halves(v):
    high = v.astype(BF)
    return high, (v - high.astype(F32)).astype(BF)


def pick(index, count):
    return (index[:, None] == jnp.arange(count, dtype=jnp.int32)[None, :]).astype(BF)


def dot(a, b):
    return jnp.dot(a, b, preferred_element_type=F32)


def hop(state, parent_row, rows_dev, replicas, me):
    grid = parent_row.reshape(replicas, rows_dev)
    source = grid // rows_dev
    local_row = grid % rows_dev
    matched = source == me
    sending = jnp.max(jnp.where(matched, local_row, 0), axis=1)
    own_source = lax.dynamic_index_in_dim(source, me, 0, keepdims=False)
    own_local = lax.dynamic_index_in_dim(local_row, me, 0, keepdims=False)
    sent = jnp.take(state, sending, axis=0)
    came = lax.all_to_all(sent, "replica", split_axis=0, concat_axis=0, tiled=True)
    rows = []
    for i in range(rows_dev):
        far = lax.dynamic_index_in_dim(came, own_source[i], 0, keepdims=True)
        near = lax.dynamic_index_in_dim(state, own_local[i], 0, keepdims=True)
        rows.append(jnp.where(own_source[i] == me, near, far))
    return jnp.concatenate(rows, axis=0)


def local(
    hidden,
    parents,
    input_weight,
    coeff_weight,
    step_weight,
    kernel_x,
    kernel_bias_x,
    kernel_coeff,
    kernel_bias_coeff,
    step_bias,
    log_rate,
    skip_gain,
    norm_gain,
    output_weight,
    scan_state,
    window_x,
    window_coeff,
):
    rows_dev, heads, head_dim, n = scan_state.shape
    steps, rows, depth = hidden.shape
    taps = kernel_x.shape[0]
    past = taps - 1
    chans = heads * head_dim
    replicas = lax.axis_size("replica")
    tensors = lax.axis_size("tensor")
    me = lax.axis_index("replica")
    mt = lax.axis_index("tensor")
    heads_all = heads * tensors
    groups = kernel_bias_coeff.shape[1] // n
    group_size = heads_all * head_dim // groups
    my_group = mt * heads * groups // heads_all
    coeff_at = my_group * n

    def own_group(v):
        return lax.dynamic_slice_in_dim(v, coeff_at, n, axis=v.ndim - 1)

    moved = scan_state.astype(BF).reshape(rows_dev, heads, head_dim, n)
    start_state = moved
    for s in range(steps):
        moved = hop(moved, parents[s], rows_dev, replicas, me)

    all_rows = jnp.arange(rows, dtype=jnp.int32)
    anc = []
    for s in range(steps):
        path = [all_rows]
        for t in range(s, -1, -1):
            path.append(jnp.take(parents[t], path[-1]))
        anc.append(path[::-1])

    def table_row(s, tau):
        if tau < past:
            return anc[s][0] * past + tau
        t = tau - past
        r = anc[s][t + 1]
        return rows * past + (r // rows_dev) * (steps * rows_dev) + t * rows_dev + r % rows_dev

    def mine(v):
        return lax.dynamic_slice_in_dim(v, me * rows_dev, rows_dev, axis=0)

    wc = own_group(window_coeff).reshape(rows_dev, past, 2 * n)
    wc_hi, wc_lo = halves(wc)
    win = jnp.concatenate([window_x.astype(BF), wc_hi, wc_lo], axis=-1)
    win = win.reshape(rows_dev * past, chans + 4 * n)
    win_all = lax.all_gather(win, "replica", axis=0, tiled=True)

    h = hidden.reshape(steps, replicas, rows_dev, depth).transpose(1, 0, 2, 3)
    h = h.reshape(steps * rows, depth)
    small_w = jnp.concatenate(
        [own_group(coeff_weight).reshape(depth, 2 * n), step_weight], axis=1
    )
    proj = dot(h, input_weight.reshape(depth, 2 * chans))
    small_w = jnp.pad(small_w, ((0, 0), (0, -small_w.shape[1] % 512)))
    small = dot(h, small_w)
    proj = lax.psum_scatter(proj, "replica", scatter_dimension=0, tiled=True)
    small = lax.psum_scatter(small, "replica", scatter_dimension=0, tiled=True)
    gate = proj[:, :chans]
    co_hi, co_lo = halves(small[:, : 2 * n])
    raw_hi, raw_lo = halves(small[:, 2 * n : 2 * n + heads])
    new = jnp.concatenate(
        [proj[:, chans : 2 * chans].astype(BF), co_hi, co_lo, raw_hi, raw_lo], axis=1
    )
    new_all = lax.all_gather(new, "replica", axis=0, tiled=True)
    wide = chans + 4 * n
    table = jnp.concatenate([win_all, new_all[:, :wide]], axis=0)
    raws = new_all[:, wide:]
    entries = table.shape[0]
    table_c = table[:, chans:]

    kern_c = own_group(kernel_coeff).reshape(taps, 2 * n)
    bias_c = own_group(kernel_bias_coeff).reshape(2 * n)

    out_c = []
    for s in range(steps):
        index = jnp.concatenate([table_row(s, s + j) for j in range(taps)])
        got = dot(pick(index, entries), table_c)
        got = (got[:, : 2 * n] + got[:, 2 * n :]).reshape(taps, rows, 2 * n)
        total = jnp.sum(got * kern_c[:, None, :], axis=0) + bias_c
        out_c.append(jax.nn.silu(total[:, n:]).reshape(replicas, 1, rows_dev, n))
    out_c = jnp.concatenate(out_c, axis=1).reshape(replicas * steps * rows_dev, n)
    home = jnp.stack([anc[s][0].reshape(replicas, rows_dev) for s in range(steps)], axis=1)
    home = home.reshape(-1)
    c_hi, c_lo = halves(out_c)
    base = jnp.zeros((2 * steps * rows, chans), F32)
    flat_state = start_state.reshape(rows_dev, chans, n)
    for q in range(rows_dev):
        here = (home == me * rows_dev + q)[:, None]
        lhs = jnp.concatenate(
            [jnp.where(here, c_hi, jnp.zeros_like(c_hi)), jnp.where(here, c_lo, jnp.zeros_like(c_lo))],
            axis=0,
        )
        base = base + lax.dot_general(
            lhs, flat_state[q], (((1,), (1,)), ((), ())), preferred_element_type=F32
        )
    base = (base[: steps * rows] + base[steps * rows :]).astype(BF)
    base = lax.psum_scatter(base, "replica", scatter_dimension=0, tiled=True).astype(F32)

    places = [(s, tau) for s in range(steps) for tau in range(s + taps)]
    index = jnp.concatenate([mine(table_row(s, tau)) for s, tau in places])
    got = dot(pick(index, entries), table)
    got_x = got[:, :chans].reshape(len(places), rows_dev, chans)
    got_c = got[:, chans : chans + 2 * n] + got[:, chans + 2 * n :]
    got_c = got_c.reshape(len(places), rows_dev, 2 * n)
    line_x = {p: got_x[k] for k, p in enumerate(places)}
    line_c = {p: got_c[k] for k, p in enumerate(places)}
    pairs = [(s, t) for s in range(steps) for t in range(s + 1)]
    index = jnp.concatenate([mine(table_row(s, t + past)) - rows * past for s, t in pairs])
    got = dot(pick(index, steps * rows), raws)
    got_raw = (got[:, :heads] + got[:, heads:]).reshape(len(pairs), rows_dev, heads)
    size = {p: jax.nn.softplus(got_raw[k] + step_bias) for k, p in enumerate(pairs)}
    rate = jnp.exp(log_rate)

    def conv(line, kern, bias, s, t):
        total = line[(s, t)] * kern[0]
        for j in range(1, taps):
            total = total + line[(s, t + j)] * kern[j]
        return jax.nn.silu(total + bias)

    norm_group = (mt * heads + jnp.arange(heads, dtype=jnp.int32)) % groups
    member = (norm_group[:, None] == jnp.arange(groups, dtype=jnp.int32)[None, :]).astype(F32)
    heads_y = []
    squares = []
    for s in range(steps):
        xs = [
            conv(line_x, kernel_x, kernel_bias_x, s, t).reshape(rows_dev, heads, head_dim)
            for t in range(s + 1)
        ]
        cs = [conv(line_c, kern_c, bias_c, s, t) for t in range(s + 1)]
        c_now = cs[s][:, n:]
        fade = jnp.ones((rows_dev, heads), F32)
        weights = [None] * (s + 1)
        for t in range(s, -1, -1):
            weights[t] = fade * size[(s, t)]
            fade = fade * jnp.exp(-rate * size[(s, t)])
        own = base[s * rows_dev : (s + 1) * rows_dev].reshape(rows_dev, heads, head_dim)
        y = fade[:, :, None] * own + skip_gain[None, :, None] * xs[s]
        for t in range(s + 1):
            match = jnp.sum(cs[t][:, :n] * c_now, axis=-1, keepdims=True)
            y = y + (weights[t] * match)[:, :, None] * xs[t]
        g = gate[s * rows_dev : (s + 1) * rows_dev].reshape(rows_dev, heads, head_dim)
        y = y * jax.nn.silu(g)
        heads_y.append(y)
        squares.append(
            jnp.dot(jnp.sum(y * y, axis=-1), member, precision=lax.Precision.HIGHEST)
        )
        if s == steps - 1:
            final = fade[:, :, None, None] * moved.astype(F32)
            for t in range(s + 1):
                final = final + (weights[t][:, :, None] * xs[t])[..., None] * (
                    cs[t][:, None, None, :n]
                )
    squares = lax.psum(jnp.concatenate(squares, axis=0), "tensor")
    inverse = lax.rsqrt(squares / group_size + 1e-05)
    head_scale = jnp.dot(inverse, member.T, precision=lax.Precision.HIGHEST)
    gains = norm_gain.reshape(heads, head_dim)
    y = jnp.concatenate(heads_y, axis=0)
    normed = (y * head_scale[:, :, None] * gains[None]).reshape(steps * rows_dev, chans)
    normed = lax.all_gather(normed.astype(BF), "replica", axis=0, tiled=True)
    mixed = lax.psum_scatter(dot(normed, output_weight), "tensor", scatter_dimension=0, tiled=True)
    width = mixed.shape[1]
    mixed = mixed.astype(BF).reshape(-1, steps, rows_dev, width).transpose(1, 0, 2, 3)
    mixed = mixed.reshape(steps, -1, width)

    last = steps - 1
    ends = [last + 1 + j for j in range(past)]
    final_x = jnp.stack([line_x[(last, tau)] for tau in ends], axis=1)
    final_c = jnp.stack([line_c[(last, tau)] for tau in ends], axis=1)
    final_c = lax.all_gather(final_c, "tensor", axis=0)
    final_c = final_c.reshape(groups, tensors // groups, rows_dev, past, 2, n)[:, 0]
    final_c = final_c.transpose(1, 2, 3, 0, 4).reshape(rows_dev, past, 2, groups * n)
    return (mixed, final, final_x, final_c)


def solution(mesh):
    placed = (
        P(None, None, "replica"),
        P(),
        P("replica", None, "tensor"),
        P("replica", None, None),
        P("replica", "tensor"),
        P(None, "tensor"),
        P("tensor"),
        P(),
        P(),
        P("tensor"),
        P("tensor"),
        P("tensor"),
        P("tensor"),
        P("tensor", "replica"),
        P("replica", "tensor", None, None),
        P("replica", None, "tensor"),
        P("replica", None, None, None),
    )
    return jax.shard_map(
        local,
        mesh=mesh,
        in_specs=placed,
        out_specs=(
            P(None, "tensor", "replica"),
            P("replica", "tensor", None, None),
            P("replica", None, "tensor"),
            P("replica", None, None, None),
        ),
        check_vma=False,
    )
```

time: 1030 us -> 539 us (0.52)
  waiting for transfers between devices: 473 us -> 0.12 us
  between operations: 15.6 us -> 121 us
  matrix products: 51.3 us -> 22.9 us
  starting transfers between devices: 41.6 us -> 16.2 us
  blocking collectives: 248 us -> 224 us
  other arithmetic: 106 us -> 86.5 us
  local copies, waits for them, and re-layouts: 78.8 us -> 60.4 us
    all_to_all x9 -> x3, waiting for transfers between devices: 378 us -> 0.01 us  [hop(): lax.all_to_all(sent, 'replica', split_axis=0, concat_axis=0, tiled=True)]
    unnamed x1 -> x0, blocking collectives: 196 us -> none
    all_gather x3 -> x4, blocking collectives: 42.8 us -> 215 us  [the longest x1 104 us: local(): new_all = lax.all_gather(new, 'replica', axis=0, tiled=True)]
    reduce_scatter x9 -> x4, waiting for transfers between devices: 95.3 us -> 0.05 us  [the longest x1 0.02 us: local(): lax.psum_scatter(base, 'replica', scatter_dimension=0, tiled=True)]
    gather x18 -> x9, local copies, waits for them, and re-layouts: 62.7 us -> 20.6 us  [the longest x3 15.9 us: hop(): sent = jnp.take(state, sending, axis=0)]
    unnamed x0 -> x21, other arithmetic: none -> 34.4 us
    concatenate x15 -> x9, other arithmetic: 39.2 us -> 7.31 us  [the longest x3 6.98 us: hop(): return jnp.concatenate(rows, axis=0)]
    reshape x9 -> x1, other arithmetic: 28.5 us -> 0.04 us  [local(): out_c.append(jax.nn.silu(total[:, n:]).reshape(replicas, 1, rows_dev, n))]
  transfers between devices with their start and end apart: 18 -> 7, of which waited for: 10 -> 0; matrix products, arithmetic and copies ran while one was open for 10% -> 22% of each run, Pallas kernels for 0% -> 0%
where the time goes in v1:
time: 539 us; the launch traced here: 531 us
  blocking collectives  224 us (42%)
  between operations  121 us (22%)
  other arithmetic  86.5 us (16%)
  local copies, waits for them, and re-layouts  60.4 us (11%)
  matrix products  22.9 us (4%)
  starting transfers between devices  16.2 us (3%)
    all_gather x1, blocking collectives, local(): new_all = lax.all_gather(new, 'replica', axis=0, tiled=True)  104 us
    all_gather x1, blocking collectives, local(): normed = lax.all_gather(normed.astype(BF), 'replica', axis=0, tiled=True)  74.5 us
    unnamed x21, other arithmetic  34.4 us
    all_gather x1, blocking collectives, local(): win_all = lax.all_gather(win, 'replica', axis=0, tiled=True)  27.2 us
    unnamed x99, local copies, waits for them, and re-layouts  16.6 us
    gather x3, local copies, waits for them, and re-layouts, hop(): sent = jnp.take(state, sending, axis=0)  15.9 us
    all_to_all x3, starting transfers between devices, hop(): lax.all_to_all(sent, 'replica', split_axis=0, concat_axis=0, tiled=True)  15.7 us
    select_n x6, other arithmetic, hop(): sent = jnp.take(state, sending, axis=0)  14 us
  transfers between devices with their start and end apart: 7, of which 0 were waited for; matrix products, arithmetic and copies ran while one was open for 22% of the time, Pallas kernels for 0%

profile of v1, /device:TPU:0, one launch (start us, length us, event | category | flops | bytes accessed | tf_op | source)
XLA Modules:
  0.0 531.5 jit_solution(8459817517178197272)
XLA Ops:
  11.4 6.5 %convert_element_type.79 = bf16[8,32,64,128]{3,2,1,0:T(8,128)(2,1)} convert(f32[8,32,64,128]{3,2,1,0:T(8,128)} %param.35) | non-fusion elementwise | flops 2097152 | bytes 12582912 | tf_op jit(solution)/shard_map/convert_element_type | solution.py:78
  17.9 5.3 gather_fusion.6
  23.2 4.7 broadcast_select_fusion.2
  27.9 6.4 %all-to-all-start = ((bf16[8,32,64,128]{3,2,1,0:T(8,128)(2,1)}), bf16[8,32,64,128]{3,2,1,0:T(8,128)(2,1)}, u32[]{:S(2)}, u32[]{:S(2)}) async-start(bf16[8,32,64,128]{3,2,1,0:T(8,128)(2,1)} %broadcast_select_fusion.2), calls=%async_computation.4 | async-start | bytes 8388608 | tf_op jit(solution)/shard_map/all_to_all | solution.py:32
  34.4 12.2 %copy.52 = bf16[128,8,2,2048]{3,1,2,0:T(8,128)(2,1)} copy(bf16[128,8,2,2048]{3,2,1,0:T(2,128)(2,1)} %bitcast.152) | data formatting | bytes 16777216
  46.6 6.8 %fusion.139 = f32[192,4096]{1,0:T(8,128)} fusion(bf16[192,1024]{1,0:T(8,128)(2,1)S(1)} %bitcast.163, bf16[1024,4096]{1,0:T(8,128)(2,1)} %bitcast.151), kind=kOutput, calls=%fused_computation.422 | convolution fusion | flops 1610612736 | bytes 11927552 | tf_op jit(solution)/shard_map/dot_general | solution.py:20
  141.5 27.2 %all_gather.16 = bf16[192,2560]{1,0:T(8,128)(2,1)S(1)} all-gather(bf16[24,2560]{1,0:T(8,128)(2,1)S(1)} %reshape.828), channel_id=1, replica_groups=mesh['replica'=8,'tensor'=4] {'replica'}, dimensions={0}, use_global_device_ids=true | all-gather | bytes 1105920 | tf_op jit(solution)/shard_map/all_gather | solution.py:105
  171.3 1.5 select_dynamic-update-slice_fusion.23
  172.9 1.4 select_dynamic-update-slice_fusion.22
  180.8 3.5 select_dynamic-update-slice_fusion.16
  184.3 2.0 copy-done.3
  186.3 5.3 gather_fusion.7
  191.6 4.7 broadcast_select_fusion.1
  196.3 4.6 all-to-all-start.1
  200.9 104.4 %all_gather.15 = bf16[192,2624]{1,0:T(8,128)(2,1)S(1)} all-gather(bf16[24,2624]{1,0:T(8,128)(2,1)S(1)} %concatenate.72), channel_id=1, replica_groups=mesh['replica'=8,'tensor'=4] {'replica'}, dimensions={0}, use_global_device_ids=true | all-gather | bytes 1133568 | tf_op jit(solution)/shard_map/all_gather | solution.py:123
  315.8 2.4 select_dynamic-update-slice_fusion.15
  318.1 2.2 select_dynamic-update-slice_fusion.14
  320.3 2.2 select_dynamic-update-slice_fusion.13
  322.5 2.0 select_dynamic-update-slice_fusion.12
  324.6 2.1 select_dynamic-update-slice_fusion.11
  326.6 2.0 select_dynamic-update-slice_fusion.10
  328.7 2.1 select_dynamic-update-slice_fusion.9
  330.7 2.1 select_dynamic-update-slice_fusion.8
  332.8 5.3 gather_fusion.8
  338.1 4.7 broadcast_select_fusion
  342.8 4.7 all-to-all-start.2
  354.0 1.4 fusion.131
  364.2 9.9 %psum.7 = f32[24,4]{0,1:T(4,128)S(1)} all-reduce(f32[24,4]{0,1:T(4,128)S(1)} %pad_maximum_fusion.5), channel_id=1, replica_groups=mesh['replica'=8,'tensor'=4] {'tensor'}, use_global_device_ids=true, to_apply=%region_15.17 | all-reduce | flops 96 | bytes 768 | tf_op jit(solution)/shard_map/psum | solution.py:212
  376.1 74.5 %all_gather.17 = bf16[192,2048]{1,0:T(8,128)(2,1)S(1)} all-gather(bf16[24,2048]{1,0:T(8,128)(2,1)S(1)} %fusion.18), channel_id=1, replica_groups=mesh['replica'=8,'tensor'=4] {'replica'}, dimensions={0}, use_global_device_ids=true | all-gather | bytes 884736 | tf_op jit(solution)/shard_map/all_gather | solution.py:218
  450.7 4.1 fusion.140
  492.2 8.4 %all-gather = f32[32,3,256]{2,0,1:T(8,128)S(1)} all-gather(f32[8,3,256]{2,0,1:T(8,128)S(1)} %pad_maximum_fusion.4), channel_id=2, replica_groups=mesh['replica'=8,'tensor'=4] {'tensor'}, dimensions={0}, use_global_device_ids=true | all-gather | bytes 122880 | tf_op jit(solution)/shard_map/all_gather | solution.py:228
  515.3 9.2 %multiply_add_fusion = f32[8,32,64,128]{3,2,1,0:T(8,128)} fusion(bf16[8,32,64,128]{3,2,1,0:T(8,128)(2,1)S(1)} %select_dynamic-update-slice_fusion, f32[8,128]{1,0:T(8,128)S(1)} %copy-done.40, f32[8,32,64]{2,1,0:T(8,128)S(1)} %broadcast_multiply_fusion, f32[8,128]{1,0:T(8,128)S(1)} %copy-done.38, f32[8,32,64]{2,1,0:T(8,128)S(1)} %get-tuple-element.86, ...), kind=kLoop, calls=%fused_computation.9 | loop fusion | flops 16777216 | bytes 12792832 | tf_op jit(solution)/shard_map/add | solution.py:209
  (328 shorter events, 74.8 us)
Async XLA Ops:
  7.2 161.5 %reduce-scatter.7.cloned.1.call-start = ((), (), s32[]{:S(2)}) async-start(), calls=%async_computation.8 | async-start | bytes 442368 | tf_op jit(solution)/shard_map/reduce_scatter | solution.py:116
  27.9 143.5 %all-to-all-start = ((bf16[8,32,64,128]{3,2,1,0:T(8,128)(2,1)}), bf16[8,32,64,128]{3,2,1,0:T(8,128)(2,1)}, u32[]{:S(2)}, u32[]{:S(2)}) async-start(bf16[8,32,64,128]{3,2,1,0:T(8,128)(2,1)} %broadcast_select_fusion.2), calls=%async_computation.4 | async-start | bytes 8388608 | tf_op jit(solution)/shard_map/all_to_all | solution.py:32
  34.2 136.0 %reduce-scatter.5.cloned.1.call-start = ((), (), s32[]{:S(2)}) async-start(), calls=%async_computation.7 | async-start | bytes 3538944 | tf_op jit(solution)/shard_map/reduce_scatter | solution.py:115
  53.5 57.4 %copy-start.18 = (f32[8,3,2048]{2,0,1:T(8,128)S(1)}, f32[8,3,2048]{2,0,1:T(8,128)}, u32[]{:S(2)}) copy-start(f32[8,3,2048]{2,0,1:T(8,128)} %param.36) | copy-start | bytes 589828
  53.5 61.0 %copy-start.41 = (f32[32]{0:T(128)S(1)}, f32[32]{0:T(128)}, u32[]{:S(2)}) copy-start(f32[32]{0:T(128)} %param.32) | copy-start | bytes 388
  53.5 61.4 %copy-start.42 = (f32[4,2,512]{2,1,0:T(2,128)S(1)}, f32[4,2,512]{2,1,0:T(2,128)}, u32[]{:S(2)}) copy-start(f32[4,2,512]{2,1,0:T(2,128)} %param.28) | copy-start | bytes 49156
  53.5 62.2 %copy-start.19 = (f32[2048]{0:T(1024)S(1)}, f32[2048]{0:T(1024)}, u32[]{:S(2)}) copy-start(f32[2048]{0:T(1024)} %param.27) | copy-start | bytes 24580
  53.5 62.8 %copy-start.34 = (f32[4,2048]{1,0:T(4,128)S(1)}, f32[4,2048]{1,0:T(4,128)}, u32[]{:S(2)}) copy-start(f32[4,2048]{1,0:T(4,128)} %param.26) | copy-start | bytes 98308
  53.5 87.9 %copy-start.45 = (f32[32]{0:T(128)S(1)}, f32[32]{0:T(128)}, u32[]{:S(2)}) copy-start(f32[32]{0:T(128)} %param.31) | copy-start | bytes 388
  116.4 239.1 %copy-start.20 = (f32[1,2048]{1,0:T(1,128)}, f32[1,2048]{1,0:T(1,128)S(1)}, u32[]{:S(2)}) copy-start(f32[1,2048]{1,0:T(1,128)S(1)} %get-tuple-element.120) | copy-start | bytes 24580
  116.4 239.1 %copy-start.21 = (f32[1,2048]{1,0:T(1,128)}, f32[1,2048]{1,0:T(1,128)S(1)}, u32[]{:S(2)}) copy-start(f32[1,2048]{1,0:T(1,128)S(1)} %get-tuple-element.121) | copy-start | bytes 24580
  171.3 4.4 copy-start.2
  196.3 119.5 %all-to-all-start.1 = ((bf16[8,32,64,128]{3,2,1,0:T(8,128)(2,1)}), bf16[8,32,64,128]{3,2,1,0:T(8,128)(2,1)}, u32[]{:S(2)}, u32[]{:S(2)}) async-start(bf16[8,32,64,128]{3,2,1,0:T(8,128)(2,1)} %broadcast_select_fusion.1), calls=%async_computation.5 | async-start | bytes 8388608 | tf_op jit(solution)/shard_map/all_to_all | solution.py:32
  200.9 151.3 %reduce-scatter.9.cloned.1.call-start = ((), (), s32[]{:S(2)}) async-start(), calls=%async_computation.9 | async-start | bytes 884736 | tf_op jit(solution)/shard_map/reduce_scatter | solution.py:156
  315.8 6.8 %copy-start.4 = (bf16[8,32,64,128]{3,2,1,0:T(8,128)(2,1)S(1)}, bf16[8,32,64,128]{3,2,1,0:T(8,128)(2,1)}, u32[]{:S(2)}) copy-start(bf16[8,32,64,128]{3,2,1,0:T(8,128)(2,1)} %copy-done.3) | copy-start | bytes 12582916
  342.8 5.1 copy-start.15
  342.8 5.4 %copy-start.43 = (f32[32]{0:T(128)S(1)}, f32[32]{0:T(128)}, u32[]{:S(2)}) copy-start(f32[32]{0:T(128)} %param.30) | copy-start | bytes 388
  342.8 10.3 %copy-start.14 = (f32[120,2560]{1,0:T(8,128)S(1)}, f32[120,2560]{1,0:T(8,128)}, u32[]{:S(2)}) copy-start(f32[120,2560]{1,0:T(8,128)} %copy-done.13) | copy-start | bytes 3686404
  342.8 161.0 %all-to-all-start.2 = ((bf16[8,32,64,128]{3,2,1,0:T(8,128)(2,1)}), bf16[8,32,64,128]{3,2,1,0:T(8,128)(2,1)}, u32[]{:S(2)}, u32[]{:S(2)}) async-start(bf16[8,32,64,128]{3,2,1,0:T(8,128)(2,1)} %broadcast_select_fusion), calls=%async_computation.6 | async-start | bytes 8388608 | tf_op jit(solution)/shard_map/all_to_all | solution.py:32
  347.5 154.7 %reduce-scatter.11.cloned.1.call-start = ((), (), s32[]{:S(2)}) async-start(), calls=%async_computation.10 | async-start | bytes 983040 | tf_op jit(solution)/shard_map/reduce_scatter | solution.py:219
  348.2 3.9 copy-start.22
  375.3 116.9 %copy-start.35 = (f32[8,1,256]{2,0,1:T(8,128)S(1)}, f32[8,1,256]{2,0,1:T(8,128)}, u32[]{:S(2)}) copy-start(f32[8,1,256]{2,0,1:T(8,128)} %get-tuple-element.93) | copy-start | bytes 24580
  375.3 116.9 %copy-start.36 = (f32[8,1,256]{2,0,1:T(8,128)S(1)}, f32[8,1,256]{2,0,1:T(8,128)}, u32[]{:S(2)}) copy-start(f32[8,1,256]{2,0,1:T(8,128)} %get-tuple-element.94) | copy-start | bytes 24580
  375.3 116.9 %copy-start.37 = (f32[8,1,256]{2,0,1:T(8,128)S(1)}, f32[8,1,256]{2,0,1:T(8,128)}, u32[]{:S(2)}) copy-start(f32[8,1,256]{2,0,1:T(8,128)} %get-tuple-element.98) | copy-start | bytes 24580
  376.1 125.3 %copy-start.16 = (f32[8,1,2048]{2,0,1:T(8,128)S(1)}, f32[8,1,2048]{2,0,1:T(8,128)}, u32[]{:S(2)}) copy-start(f32[8,1,2048]{2,0,1:T(8,128)} %get-tuple-element.76) | copy-start | bytes 196612
  376.1 125.3 %copy-start.17 = (f32[8,1,2048]{2,0,1:T(8,128)S(1)}, f32[8,1,2048]{2,0,1:T(8,128)}, u32[]{:S(2)}) copy-start(f32[8,1,2048]{2,0,1:T(8,128)} %get-tuple-element.77) | copy-start | bytes 196612
  376.1 126.0 %copy-start.33 = (f32[8,32]{1,0:T(8,128)S(1)}, f32[8,32]{1,0:T(8,128)}, u32[]{:S(2)}) copy-start(f32[8,32]{1,0:T(8,128)} %copy-done.32) | copy-start | bytes 3076
  508.1 7.2 %copy-start.23 = (f32[8,32]{1,0:T(8,128)S(1)}, f32[8,32]{1,0:T(8,128)}, u32[]{:S(2)}) copy-start(f32[8,32]{1,0:T(8,128)} %copy-done.22) | copy-start | bytes 3076
  508.1 7.2 %copy-start.38 = (f32[8,128]{1,0:T(8,128)S(1)}, f32[8,128]{1,0:T(8,128)}, u32[]{:S(2)}) copy-start(f32[8,128]{1,0:T(8,128)} %get-tuple-element.36) | copy-start | bytes 12292
  508.1 7.2 %copy-start.39 = (f32[8,128]{1,0:T(8,128)S(1)}, f32[8,128]{1,0:T(8,128)}, u32[]{:S(2)}) copy-start(f32[8,128]{1,0:T(8,128)} %get-tuple-element.37) | copy-start | bytes 12292
  508.1 7.2 %copy-start.40 = (f32[8,128]{1,0:T(8,128)S(1)}, f32[8,128]{1,0:T(8,128)}, u32[]{:S(2)}) copy-start(f32[8,128]{1,0:T(8,128)} %get-tuple-element.145) | copy-start | bytes 12292
  515.3 9.2 %copy-start.1 = (bf16[1024,2,512]{2,1,0:T(2,128)(2,1)S(1)}, bf16[1024,2,512]{2,1,0:T(2,128)(2,1)}, u32[]{:S(2)}) copy-start(bf16[1024,2,512]{2,1,0:T(2,128)(2,1)} %param.24) | copy-start | bytes 6291460
  (21 other events, 40.1 us)
Sparse Core Ops, SparseCore 0:
  11.2 34.0 reduce-scatter.6
  53.7 89.3 reduce-scatter.4
  315.9 32.4 reduce-scatter.8
  455.0 26.7 reduce-scatter.10
